TPU v7x, 32 devices: a whole 2x2x4 slice. The times are simulated.
32 devices in a mesh: tm: 4 (over y, x), tile: 8 (over z, core).
Axes of the slice: x: 2, y: 2, z: 4, core: 2. Of those that a mesh axis runs over, the one named last changes fastest.
Arguments:
- diag_blocks: float32 [16384, 4096], P(('tm', 'tile')), as said below
- coupling: float32 [16384, 4096], P(('tm', 'tile')), as said below
- next_diag: float32 [16384, 4096], P(('tm', 'tile')), as said below
- arrow_now: float32 [128, 4096], P('tm'), may hold values from -0.4375 to 0.4375
- arrow_next: float32 [128, 4096], P('tm'), may hold values from -0.4375 to 0.4375
- arrow_tip: float32 [128, 32], P('tm'), may hold values from -6 to 6
Outputs:
- factor_lower: float32 [16384, 4096], P(('tm', 'tile'))
- coupling_out: float32 [16384, 4096], P(('tm', 'tile'))
- arrow_factor: float32 [128, 4096], P('tm')
- handed_diag: float32 [16384, 4096], P(('tm', 'tile'))
- handed_arrow: float32 [128, 4096], P('tm')
- handed_tip: float32 [128, 32], P('tm')
Inputs may be any that keep to these rules, and one draw needn't show every extreme that they name: `diag_blocks`: each 4096 x 4096 block is symmetric positive definite. `next_diag`: each 4096 x 4096 block is symmetric positive definite. `coupling`: with the diag_blocks block and the next_diag block of its time step, each 4096 x 4096 block forms a symmetric positive definite two-block precision matrix.
All inputs are finite; a program needn't handle non-finite values.
Results may differ from a plain program's by a relative error of at most 0.0001.
Values sent between devices are 32-bit elements; how exact they have to be, the bound alone decides.
No kernel may reach another device: no remote copies, remote signals or barrier semaphores. Data moves between devices by JAX's collectives and lax.ppermute only.
A program may use at most 256 MiB of HBM per device.

v0:
```python
import jax
import jax.numpy as jnp
from jax import lax
from jax.sharding import PartitionSpec as P

precise = lax.Precision.HIGHEST


def broadcast(block, axis, source):
    block = jnp.where(lax.axis_index(axis) == source, block, jnp.zeros_like(block))
    return lax.psum(block, axis)


def shifted(value, axis, steps):
    count = lax.axis_size(axis)
    leading, last = (max(0, -steps), min(count, count - steps))
    return lax.ppermute(value, axis, [(source, source + steps) for source in range(leading, last)])


def outer_rows(left_rows, right_rows):
    return lax.dot_general(
        left_rows,
        right_rows,
        (((1,), (1,)), ((), ())),
        precision=precise,
        preferred_element_type=jnp.float32,
    )


def solve_rows(factor, block):
    return jax.scipy.linalg.solve_triangular(factor, block.T, lower=True).T


def local(diag_blocks, coupling, next_diag, arrow_now, arrow_next, arrow_tip):
    row_count = diag_blocks.shape[0]
    col_count = diag_blocks.shape[1]
    panels = lax.axis_size("tile") // 4
    my_index = lax.axis_index("tile")
    row_ids = my_index * row_count + lax.iota(jnp.int32, row_count)
    work_a, work_c, arrow_a = (diag_blocks, coupling, arrow_now)
    next_d, arrow_b, tip_block = (next_diag, arrow_next, arrow_tip)
    for number in range(panels):
        offset = number * row_count
        factor_offset = number * row_count
        factor_ending = factor_offset + row_count
        pivot_blk = broadcast(work_a[:, factor_offset:factor_ending], "tile", number)
        factor = jnp.linalg.cholesky(pivot_blk)
        factor_local_a = jnp.where(
            (row_ids >= factor_offset)[:, None],
            solve_rows(factor, work_a[:, factor_offset:factor_ending]),
            0.0,
        )
        factor_local_c = solve_rows(factor, work_c[:, factor_offset:factor_ending])
        factor_whole_a = lax.all_gather(factor_local_a, "tile", axis=0, tiled=True)
        factor_whole_c = lax.all_gather(factor_local_c, "tile", axis=0, tiled=True)
        factor_local_r = solve_rows(factor, arrow_a[:, factor_offset:factor_ending])
        panel_k = (
            factor_offset,
            factor_local_a,
            factor_local_c,
            factor_local_r,
            factor_whole_a,
            factor_whole_c,
        )
        store_work_a = work_a
        store_work_c = work_c
        store_arrow_a = arrow_a
        store_offset = panel_k[0]
        store_local_a = panel_k[1]
        store_local_c = panel_k[2]
        store_local_r = panel_k[3]
        ending = store_offset + row_count
        store_work_a = store_work_a.at[:, store_offset:ending].set(store_local_a)
        store_work_c = store_work_c.at[:, store_offset:ending].set(store_local_c)
        store_arrow_a = store_arrow_a.at[:, store_offset:ending].set(store_local_r)
        work_a = store_work_a
        work_c = store_work_c
        arrow_a = store_arrow_a
        col_lo = offset + row_count
        apply_work_a = work_a
        apply_work_c = work_c
        apply_arrow_a = arrow_a
        apply_offset = panel_k[0]
        local_a = panel_k[1]
        apply_local_c = panel_k[2]
        apply_local_r = panel_k[3]
        whole_a = panel_k[4]
        keep_rows = (row_ids >= apply_offset + row_count)[:, None]
        targets = whole_a[col_lo:col_count]
        apply_work_a = apply_work_a.at[:, col_lo:col_count].add(
            -jnp.where(keep_rows, outer_rows(local_a, targets), 0.0)
        )
        apply_work_c = apply_work_c.at[:, col_lo:col_count].add(-outer_rows(apply_local_c, targets))
        apply_arrow_a = apply_arrow_a.at[:, col_lo:col_count].add(
            -outer_rows(apply_local_r, targets)
        )
        work_a = apply_work_a
        work_c = apply_work_c
        arrow_a = apply_arrow_a
        apply_next_d = next_d
        apply_arrow_b = arrow_b
        apply_tip_block = tip_block
        local_c = panel_k[2]
        local_r = panel_k[3]
        whole_c = panel_k[5]
        apply_next_d = apply_next_d - outer_rows(local_c, whole_c)
        apply_arrow_b = apply_arrow_b - outer_rows(local_r, whole_c)
        apply_tip_block = apply_tip_block - outer_rows(local_r, local_r)
        next_d = apply_next_d
        arrow_b = apply_arrow_b
        tip_block = apply_tip_block
    col_ids = lax.iota(jnp.int32, col_count)
    factor_lower = jnp.where(col_ids[None, :] <= row_ids[:, None], work_a, 0.0)
    handed_diag, handed_arrow, handed_tip = shifted((next_d, arrow_b, tip_block), "tm", 1)
    return (factor_lower, work_c, arrow_a, handed_diag, handed_arrow, handed_tip)


def solution(mesh):
    return jax.shard_map(
        local,
        mesh=mesh,
        in_specs=(
            P(("tm", "tile"), None),
            P(("tm", "tile"), None),
            P(("tm", "tile"), None),
            P("tm", None),
            P("tm", None),
            P("tm", None),
        ),
        out_specs=(
            P(("tm", "tile"), None),
            P(("tm", "tile"), None),
            P("tm", None),
            P(("tm", "tile"), None),
            P("tm", None),
            P("tm", None),
        ),
        check_vma=False,
    )
```

profile of v0, /device:TPU:0, one launch (start us, length us, event | category | flops | bytes accessed | tf_op | source)
XLA Modules:
  0.0 914.3 jit_solution(8446192928893483997)
XLA Ops:
  7.2 7.9 copy.105
  22.5 61.0 %all-reduce.4.cloned.1.call-done = f32[512,512]{1,0:T(8,128)} async-done(((f32[512,512]{1,0:T(8,128)}), f32[512,512]{1,0:T(8,128)}) %all-reduce.4.cloned.1.call-update) | async-done | bytes 1048592 | tf_op jit(solution)/shard_map/psum | solution.py:11
  86.6 11.7 %cholesky.286 = f32[128,128]{1,0:T(8,128)S(1)} custom-call(f32[128,128]{1,0:T(8,128)S(1)} %copy.14), custom_call_target="Cholesky" | custom-call | tf_op jit(solution)/shard_map/jit(cholesky)/cholesky | solution.py:47
  98.4 9.8 %custom-call.33 = f32[1,128,128]{1,2,0:T(8,128)S(1)} custom-call(f32[1,128,128]{2,1,0:T(8,128)S(1)} %get-tuple-element.246), custom_call_target="InvertDiagBlocksLowerTriangular" | custom-call | tf_op jit(solution)/shard_map/jit(cholesky)/cholesky | solution.py:47
  109.3 11.7 %cholesky.305 = f32[128,128]{1,0:T(8,128)S(1)} custom-call(f32[128,128]{1,0:T(8,128)S(1)} %copy.16), custom_call_target="Cholesky" | custom-call | tf_op jit(solution)/shard_map/jit(cholesky)/cholesky | solution.py:47
  121.1 10.0 %custom-call.34 = f32[1,128,128]{1,2,0:T(8,128)S(1)} custom-call(f32[1,128,128]{2,1,0:T(8,128)S(1)} %get-tuple-element.243), custom_call_target="InvertDiagBlocksLowerTriangular" | custom-call | tf_op jit(solution)/shard_map/jit(cholesky)/cholesky | solution.py:47
  132.0 11.7 %cholesky.326 = f32[128,128]{1,0:T(8,128)S(1)} custom-call(f32[128,128]{1,0:T(8,128)S(1)} %copy.18), custom_call_target="Cholesky" | custom-call | tf_op jit(solution)/shard_map/jit(cholesky)/cholesky | solution.py:47
  144.4 9.8 %custom-call.35 = f32[1,128,128]{1,2,0:T(8,128)S(1)} custom-call(f32[1,128,128]{2,1,0:T(8,128)S(1)} %get-tuple-element.240), custom_call_target="InvertDiagBlocksLowerTriangular" | custom-call | tf_op jit(solution)/shard_map/jit(cholesky)/cholesky | solution.py:47
  155.0 12.2 %cholesky.343 = f32[128,128]{1,0:T(8,128)S(1)} custom-call(f32[128,128]{1,0:T(8,128)S(1)} %copy.20), custom_call_target="Cholesky" | custom-call | tf_op jit(solution)/shard_map/jit(cholesky)/cholesky | solution.py:47
  178.9 39.3 %custom-call.36 = f32[4,128,128]{1,2,0:T(8,128)S(1)} custom-call(f32[4,128,128]{2,1,0:T(8,128)S(1)} %get-tuple-element.193), custom_call_target="InvertDiagBlocksLowerTriangular" | custom-call | tf_op jit(solution)/shard_map/jit(_solve_triangular)/triangular_solve | solution.py:31
  237.6 73.9 %all-gather.5.cloned.1.call-done = f32[4096,512]{1,0:T(8,128)} async-done(((f32[512,512]{1,0:T(8,128)}), f32[4096,512]{1,0:T(8,128)}) %all-gather.5.cloned.1.call-update) | async-done | bytes 8388624 | tf_op jit(solution)/shard_map/all_gather | solution.py:54
  311.4 17.8 %constant_dynamic-update-slice_fusion.4 = (f32[512,4096]{1,0:T(8,128)}, f32[512,3584]{1,0:T(8,128)S(1)}) fusion(f32[512,4096]{1,0:T(8,128)} %get-tuple-element.217, f32[4096,512]{1,0:T(8,128)} %all-gather.5.cloned.1.call-done, f32[128,512]{0,1:T(8,128)} %copy-done.17, f32[128,512]{0,1:T(8,128)} %copy-done.16, f32[128,512]{0,1:T(8,128)} %copy-done.15, ...), kind=kOutput, calls=%fused_computation.244 | convolution fusion | flops 11280842752 | bytes 30409728 | tf_op jit(solution)/shard_map/dot_general | solution.py:21
  344.0 17.6 %constant_dynamic-update-slice_fusion.3 = (f32[512,4096]{1,0:T(8,128)}, f32[512,3584]{1,0:T(8,128)S(1)}) fusion(f32[512,4096]{1,0:T(8,128)} %select_dynamic-update-slice_fusion.1, f32[4096,512]{1,0:T(8,128)} %all-gather.5.cloned.1.call-done, f32[128,512]{0,1:T(8,128)S(1)} %fusion.130, f32[128,512]{0,1:T(8,128)S(1)} %copy.33, f32[128,512]{0,1:T(8,128)S(1)} %copy.32, ...), kind=kOutput, calls=%fused_computation.243 | convolution fusion | flops 11278745600 | bytes 30408704 | tf_op jit(solution)/shard_map/dot_general | solution.py:21
  365.6 28.9 %all-reduce.6.cloned.1.call-done = f32[512,512]{0,1:T(8,128)} async-done(((f32[512,512]{0,1:T(8,128)}), f32[512,512]{0,1:T(8,128)}) %all-reduce.6.cloned.1.call-update) | async-done | bytes 1048592 | tf_op jit(solution)/shard_map/psum | solution.py:11
  398.5 11.7 %cholesky.358 = f32[128,128]{1,0:T(8,128)S(1)} custom-call(f32[128,128]{1,0:T(8,128)S(1)} %cholesky.439), custom_call_target="Cholesky" | custom-call | tf_op jit(solution)/shard_map/jit(cholesky)/cholesky | solution.py:47
  410.2 9.8 %custom-call.37 = f32[1,128,128]{1,2,0:T(8,128)S(1)} custom-call(f32[1,128,128]{2,1,0:T(8,128)S(1)} %get-tuple-element.236), custom_call_target="InvertDiagBlocksLowerTriangular" | custom-call | tf_op jit(solution)/shard_map/jit(cholesky)/cholesky | solution.py:47
  423.4 11.7 %cholesky.377 = f32[128,128]{1,0:T(8,128)S(1)} custom-call(f32[128,128]{1,0:T(8,128)S(1)} %cholesky.443), custom_call_target="Cholesky" | custom-call | tf_op jit(solution)/shard_map/jit(cholesky)/cholesky | solution.py:47
  435.1 9.9 %custom-call.38 = f32[1,128,128]{1,2,0:T(8,128)S(1)} custom-call(f32[1,128,128]{2,1,0:T(8,128)S(1)} %get-tuple-element.233), custom_call_target="InvertDiagBlocksLowerTriangular" | custom-call | tf_op jit(solution)/shard_map/jit(cholesky)/cholesky | solution.py:47
  447.5 11.7 %cholesky.398 = f32[128,128]{1,0:T(8,128)S(1)} custom-call(f32[128,128]{1,0:T(8,128)S(1)} %cholesky.448), custom_call_target="Cholesky" | custom-call | tf_op jit(solution)/shard_map/jit(cholesky)/cholesky | solution.py:47
  459.3 9.8 %custom-call.39 = f32[1,128,128]{1,2,0:T(8,128)S(1)} custom-call(f32[1,128,128]{2,1,0:T(8,128)S(1)} %get-tuple-element.230), custom_call_target="InvertDiagBlocksLowerTriangular" | custom-call | tf_op jit(solution)/shard_map/jit(cholesky)/cholesky | solution.py:47
  470.5 11.7 %cholesky.415 = f32[128,128]{1,0:T(8,128)S(1)} custom-call(f32[128,128]{1,0:T(8,128)S(1)} %convolution_subtract_fusion.18), custom_call_target="Cholesky" | custom-call | tf_op jit(solution)/shard_map/jit(cholesky)/cholesky | solution.py:47
  488.9 11.9 %while.25 = (s32[]{:T(128)}, f32[512,512]{1,0:T(8,128)}, s32[4,2]{0,1:T(2,128)S(1)}, f32[4,128,128]{2,1,0:T(8,128)S(1)}, s32[]{:T(128)}) while((s32[]{:T(128)}, f32[512,512]{1,0:T(8,128)}, s32[4,2]{0,1:T(2,128)S(1)}, f32[4,128,128]{2,1,0:T(8,128)S(1)}, s32[]{:T(128)}) %tuple.143), condition=%wide.while_cond.12.clone, body=%wide.while_body.12.clone.sunk | while | flops 2 | bytes 131189 | solution.py:31
  500.8 39.3 %custom-call.40 = f32[4,128,128]{1,2,0:T(8,128)S(1)} custom-call(f32[4,128,128]{2,1,0:T(8,128)S(1)} %get-tuple-element.194), custom_call_target="InvertDiagBlocksLowerTriangular" | custom-call | tf_op jit(solution)/shard_map/jit(_solve_triangular)/triangular_solve | solution.py:31
  579.8 17.3 %fusion.92 = f32[512,4096]{1,0:T(8,128)} fusion(f32[4096,512]{1,0:T(8,128)} %all-gather.9.cloned.1.call-done, f32[128,512]{0,1:T(8,128)S(1)} %fusion.130, f32[128,512]{0,1:T(8,128)S(1)} %copy.33, f32[128,512]{0,1:T(8,128)S(1)} %copy.32, f32[128,512]{0,1:T(8,128)S(1)} %copy.31), kind=kOutput, calls=%fused_computation.136 | convolution fusion | flops 12885688320 | bytes 17825792 | tf_op jit(solution)/shard_map/dot_general | solution.py:21
  597.0 37.2 %all-gather.11.cloned.1.call-done = f32[4096,512]{1,0:T(8,128)} async-done(((f32[512,512]{1,0:T(8,128)}), f32[4096,512]{1,0:T(8,128)}) %all-gather.11.cloned.1.call-update) | async-done | bytes 8388624 | tf_op jit(solution)/shard_map/all_gather | solution.py:55
  634.2 21.0 %subtract_subtract_fusion = f32[512,4096]{1,0:T(8,128)} fusion(f32[512,4096]{1,0:T(8,128)} %param.37, f32[512,4096]{1,0:T(8,128)} %fusion.92, f32[4096,512]{1,0:T(8,128)} %all-gather.11.cloned.1.call-done, f32[128,512]{0,1:T(8,128)S(1)} %fusion.140, f32[128,512]{0,1:T(8,128)S(1)} %copy.37, f32[128,512]{0,1:T(8,128)S(1)} %copy.36, f32[128,512]{0,1:T(8,128)S(1)} %copy.35), kind=kOutput, calls=%fused_computation.4 | convolution fusion | flops 12889882624 | bytes 34603008 | tf_op jit(solution)/shard_map/dot_general | solution.py:21
  664.0 9.2 %fusion.21 = f32[32,3584]{1,0:T(8,128)S(1)} fusion(f32[4096,512]{1,0:T(8,128)} %all-gather.5.cloned.1.call-done, f32[32,4096]{1,0:T(8,128)S(1)} %fusion.115, f32[128,32]{0,1:T(8,128)S(1)} %fusion.129, f32[128,32]{0,1:T(8,128)S(1)} %fusion.126, f32[128,32]{0,1:T(8,128)S(1)} %fusion.123, f32[128,32]{0,1:T(8,128)S(1)} %fusion.122), kind=kOutput, calls=%fused_computation.27 | convolution fusion | flops 704921600 | bytes 8323072 | tf_op jit(solution)/shard_map/dot_general | solution.py:21
  690.5 149.0 %collective-permute-done.2 = f32[32,32]{1,0:T(8,128)S(1)} collective-permute-done((f32[32,32]{1,0:T(8,128)S(1)}, f32[32,32]{1,0:T(8,128)S(1)}, u32[]{:S(2)}, u32[]{:S(2)}) %collective-permute-start.2) | collective-permute-done | bytes 4128 | tf_op jit(solution)/shard_map/ppermute | solution.py:17
  852.7 15.2 %fusion.7 = f32[512,4096]{1,0:T(8,128)} fusion(f32[512,4096]{1,0:T(8,128)} %get-tuple-element.215, f32[4096,512]{1,0:T(8,128)} %all-gather.7.cloned.1.call-done, pred[512]{0:T(512)(128)(4,1)S(1)} %fusion.166, f32[128,512]{0,1:T(8,128)S(1)} %copy-done.13, f32[128,512]{0,1:T(8,128)S(1)} %copy-done.11, f32[128,512]{0,1:T(8,128)S(1)} %copy-done.10, ...), kind=kOutput, calls=%fused_computation.17 | convolution fusion | flops 9669443584 | bytes 19923968 | tf_op jit(solution)/shard_map/dot_general | solution.py:21
  867.9 8.8 fusion
  876.7 14.0 %fusion.6 = f32[512,4096]{1,0:T(8,128)} fusion(f32[512,4096]{1,0:T(8,128)} %select_dynamic-update-slice_fusion, f32[4096,512]{1,0:T(8,128)S(1)} %copy-done, f32[128,512]{0,1:T(8,128)S(1)} %fusion.140, f32[128,512]{0,1:T(8,128)S(1)} %copy.37, f32[128,512]{0,1:T(8,128)S(1)} %copy.36, f32[128,512]{0,1:T(8,128)S(1)} %copy.35), kind=kOutput, calls=%fused_computation.15 | convolution fusion | flops 9667608576 | bytes 19922944 | tf_op jit(solution)/shard_map/dot_general | solution.py:21
  896.5 8.0 copy.109
  (238 shorter events, 182.3 us)
Async XLA Ops:
  7.2 76.3 %all-reduce.4.cloned.1.call-start = ((), (), s32[]{:S(2)}) async-start(), calls=%async_computation | async-start | bytes 2097152 | tf_op jit(solution)/shard_map/psum | solution.py:11
  7.2 7.9 copy-start.4
  21.8 289.6 %all-gather.5.cloned.1.call-start = ((), (), s32[]{:S(2)}) async-start(), calls=%async_computation.1 | async-start | bytes 9437184 | tf_op jit(solution)/shard_map/all_gather | solution.py:54
  218.2 6.0 copy-start.18
  218.8 11.5 %copy-start.14 = (f32[128,512]{0,1:T(8,128)}, f32[128,512]{0,1:T(8,128)S(1)}, u32[]{:S(2)}) copy-start(f32[128,512]{0,1:T(8,128)S(1)} %copy.21) | copy-start | bytes 786436
  219.9 10.4 %copy-start.15 = (f32[128,512]{0,1:T(8,128)}, f32[128,512]{0,1:T(8,128)S(1)}, u32[]{:S(2)}) copy-start(f32[128,512]{0,1:T(8,128)S(1)} %copy.22) | copy-start | bytes 786436
  225.3 5.0 copy-start.16
  225.3 8.4 copy-start.19
  226.8 3.5 copy-start.17
  230.3 164.2 %all-reduce.6.cloned.1.call-start = ((), (), s32[]{:S(2)}) async-start(), calls=%async_computation.2 | async-start | bytes 2097152 | tf_op jit(solution)/shard_map/psum | solution.py:11
  231.7 97.6 %copy-start.7 = (f32[512,512]{0,1:T(8,128)}, f32[512,512]{0,1:T(8,128)S(1)}, u32[]{:S(2)}) copy-start(f32[512,512]{0,1:T(8,128)S(1)} %slice_bitcast_fusion.1) | copy-start | bytes 3145732
  336.1 243.6 %all-gather.9.cloned.1.call-start = ((), (), s32[]{:S(2)}) async-start(), calls=%async_computation.4 | async-start | bytes 9437184 | tf_op jit(solution)/shard_map/all_gather | solution.py:55
  341.0 293.2 %all-gather.11.cloned.1.call-start = ((), (), s32[]{:S(2)}) async-start(), calls=%async_computation.5 | async-start | bytes 9437184 | tf_op jit(solution)/shard_map/all_gather | solution.py:55
  540.2 5.8 copy-start.20
  553.1 299.6 %all-gather.7.cloned.1.call-start = ((), (), s32[]{:S(2)}) async-start(), calls=%async_computation.3 | async-start | bytes 9437184 | tf_op jit(solution)/shard_map/all_gather | solution.py:54
  571.5 8.3 copy-start.12
  597.0 66.1 %copy-start.26 = (f32[32,32]{1,0:T(8,128)S(1)}, f32[32,32]{1,0:T(8,128)}, u32[]{:S(2)}) copy-start(f32[32,32]{1,0:T(8,128)} %param.40) | copy-start | bytes 12292
  597.0 66.3 %copy-start.5 = (f32[32,4096]{1,0:T(8,128)S(1)}, f32[32,4096]{1,0:T(8,128)}, u32[]{:S(2)}) copy-start(f32[32,4096]{1,0:T(8,128)} %copy.107) | copy-start | bytes 1572868
  655.2 18.1 %copy-start.1 = (f32[4096,512]{1,0:T(8,128)S(1)}, f32[4096,512]{1,0:T(8,128)}, u32[]{:S(2)}) copy-start(f32[4096,512]{1,0:T(8,128)} %all-gather.9.cloned.1.call-done) | copy-start | bytes 25165828
  655.2 18.1 %copy-start.24 = (f32[32,4096]{1,0:T(8,128)S(1)}, f32[32,4096]{1,0:T(8,128)}, u32[]{:S(2)}) copy-start(f32[32,4096]{1,0:T(8,128)} %param.39) | copy-start | bytes 1572868
  655.2 241.3 %collective-permute-start = (f32[512,4096]{1,0:T(8,128)}, f32[512,4096]{1,0:T(8,128)}, u32[]{:S(2)}, u32[]{:S(2)}) collective-permute-start(f32[512,4096]{1,0:T(8,128)} %subtract_subtract_fusion), channel_id=1, source_target_pairs={{0,8},{8,16},{16,24},{1,9},{9,17},{17,25},{2,10},{10,18},{18,26},{... | collective-permute-start | bytes 25165832 | tf_op jit(solution)/shard_map/ppermute | solution.py:17
  664.0 17.0 %copy-start.21 = (f32[4,128,128]{1,2,0:T(8,128)S(1)}, f32[4,128,128]{1,2,0:T(8,128)}, u32[]{:S(2)}) copy-start(f32[4,128,128]{1,2,0:T(8,128)} %copy-done.20) | copy-start | bytes 786436
  664.0 175.5 %slice-start = ((s8[8388608]{0:T(1024)(128)(4,1)}), s8[4194304]{0:T(1024)(128)(4,1)S(1)}, s32[]{:S(2)}) async-start(s8[8388608]{0:T(1024)(128)(4,1)} %bitcast.194), calls=%async_computation.6 | async-start | bytes 8388608
  673.4 166.2 %slice-start.1 = ((s8[8388608]{0:T(1024)(128)(4,1)}), s8[4194304]{0:T(1024)(128)(4,1)S(1)}, s32[]{:S(2)}) async-start(s8[8388608]{0:T(1024)(128)(4,1)} %bitcast.194), calls=%async_computation.7 | async-start | bytes 8388608
  681.0 171.7 %copy-start.9 = (f32[128,512]{0,1:T(8,128)S(1)}, f32[128,512]{0,1:T(8,128)}, u32[]{:S(2)}) copy-start(f32[128,512]{0,1:T(8,128)} %copy.27) | copy-start | bytes 786436
  681.0 171.7 %copy-start.10 = (f32[128,512]{0,1:T(8,128)S(1)}, f32[128,512]{0,1:T(8,128)}, u32[]{:S(2)}) copy-start(f32[128,512]{0,1:T(8,128)} %copy.28) | copy-start | bytes 786436
  681.0 171.7 %copy-start.11 = (f32[128,512]{0,1:T(8,128)S(1)}, f32[128,512]{0,1:T(8,128)}, u32[]{:S(2)}) copy-start(f32[128,512]{0,1:T(8,128)} %copy.29) | copy-start | bytes 786436
  681.0 171.7 %copy-start.13 = (f32[128,512]{0,1:T(8,128)S(1)}, f32[128,512]{0,1:T(8,128)}, u32[]{:S(2)}) copy-start(f32[128,512]{0,1:T(8,128)} %copy-done.12) | copy-start | bytes 786436
  685.5 154.0 %collective-permute-start.2 = (f32[32,32]{1,0:T(8,128)S(1)}, f32[32,32]{1,0:T(8,128)S(1)}, u32[]{:S(2)}, u32[]{:S(2)}) collective-permute-start(f32[32,32]{1,0:T(8,128)S(1)} %convolution_subtract_fusion.20), channel_id=1, source_target_pairs={{0,8},{8,16},{16,24},{1,9},{9,17},{17,25},{2,10},{10,18},{18,26},{... | collective-permute-start | bytes 12296 | tf_op jit(solution)/shard_map/ppermute | solution.py:17
  847.2 49.3 %collective-permute-start.1 = (f32[32,4096]{1,0:T(8,128)S(1)}, f32[32,4096]{1,0:T(8,128)}, u32[]{:S(2)}, u32[]{:S(2)}) collective-permute-start(f32[32,4096]{1,0:T(8,128)S(1)} %convolution_subtract_fusion), channel_id=1, source_target_pairs={{0,8},{8,16},{16,24},{1,9},{9,17},{17,25},{2,10},{10,18},{18,26},{... | collective-permute-start | bytes 1572872 | tf_op jit(solution)/shard_map/ppermute | solution.py:17
  867.9 8.8 copy-start
  896.5 8.0 copy-start.6
  (6 other events, 11.7 us)
Sparse Core Ops, SparseCore 0:
  22.0 61.4 all-reduce.3
  230.4 81.0 all-gather.4
  336.3 58.1 all-reduce.5
  395.9 81.0 all-gather.8
  553.2 80.9 all-gather.10
  635.7 80.5 all-gather.6
where the time goes:
time: 926 us; the launch traced here: 914 us
  waiting for transfers between devices  350 us (38%)
  other arithmetic  271 us (29%)
  matrix products  189 us (20%)
  local copies, waits for them, and re-layouts  68.5 us (7%)
  between operations  20.9 us (2%)
  starting transfers between devices  14.1 us (2%)
    another operation x29, other arithmetic, local(): factor = jnp.linalg.cholesky(pivot_blk)  158 us
    ppermute x3, waiting for transfers between devices, shifted(): lax.ppermute(value, axis, [(source, source + steps) for source in range(l...  149 us
    dot_general x12, matrix products, outer_rows(): lax.dot_general(left_rows, right_rows, (((1,), (1,)), ((), ())), precisio...  134 us
    psum x2, waiting for transfers between devices, broadcast(): return lax.psum(block, axis)  89.8 us
    another operation x5, other arithmetic, solve_rows(): return jax.scipy.linalg.solve_triangular(factor, block.T, lower=True).T  79.9 us
    all_gather x2, waiting for transfers between devices, local(): factor_whole_a = lax.all_gather(factor_local_a, 'tile', axis=0, tiled=True)  73.9 us
    another operation x42, matrix products, solve_rows(): return jax.scipy.linalg.solve_triangular(factor, block.T, lower=True).T  47 us
    all_gather x2, waiting for transfers between devices, local(): factor_whole_c = lax.all_gather(factor_local_c, 'tile', axis=0, tiled=True)  37.2 us
  transfers between devices with their start and end apart: 9, of which 5 were waited for; matrix products, arithmetic and copies ran while one was open for 36% of the time, Pallas kernels for 0%

commit v1 on v0

--- a/solution.py
+++ b/solution.py
@@ -51,8 +51,16 @@
             0.0,
         )
         factor_local_c = solve_rows(factor, work_c[:, factor_offset:factor_ending])
-        factor_whole_a = lax.all_gather(factor_local_a, "tile", axis=0, tiled=True)
-        factor_whole_c = lax.all_gather(factor_local_c, "tile", axis=0, tiled=True)
+        factor_whole_a, factor_whole_c = jnp.split(
+            lax.all_gather(
+                jnp.concatenate([factor_local_a, factor_local_c], axis=1),
+                "tile",
+                axis=0,
+                tiled=True,
+            ),
+            [factor_local_a.shape[1]],
+            axis=1,
+        )
         factor_local_r = solve_rows(factor, arrow_a[:, factor_offset:factor_ending])
         panel_k = (
             factor_offset,

time: 926 us -> 1120 us (1.21)
  waiting for transfers between devices: 350 us -> 545 us
    all_gather x4 -> x2, waiting for transfers between devices: 111 us -> 292 us  [local(): lax.all_gather(jnp.concatenate([factor_local_a, factor_local_c], axis=1),...]
    unnamed x64 -> x52, local copies, waits for them, and re-layouts: 30.9 us -> 29.9 us
  transfers between devices with their start and end apart: 9 -> 7, of which waited for: 5 -> 5; matrix products, arithmetic and copies ran while one was open for 36% -> 10% of each run, Pallas kernels for 0% -> 0%
where the time goes in v1:
time: 1120 us; the launch traced here: 1110 us
  waiting for transfers between devices  545 us (49%)
  other arithmetic  267 us (24%)
  matrix products  196 us (18%)
  local copies, waits for them, and re-layouts  64.8 us (6%)
  between operations  20.4 us (2%)
  starting transfers between devices  12.6 us (1%)
    all_gather x2, waiting for transfers between devices, local(): lax.all_gather(jnp.concatenate([factor_local_a, factor_local_c], axis=1),...  292 us
    another operation x29, other arithmetic, local(): factor = jnp.linalg.cholesky(pivot_blk)  158 us
    ppermute x3, waiting for transfers between devices, shifted(): lax.ppermute(value, axis, [(source, source + steps) for source in range(l...  158 us
    dot_general x12, matrix products, outer_rows(): lax.dot_general(left_rows, right_rows, (((1,), (1,)), ((), ())), precisio...  140 us
    psum x2, waiting for transfers between devices, broadcast(): return lax.psum(block, axis)  95.3 us
    another operation x5, other arithmetic, solve_rows(): return jax.scipy.linalg.solve_triangular(factor, block.T, lower=True).T  79.9 us
    another operation x42, matrix products, solve_rows(): return jax.scipy.linalg.solve_triangular(factor, block.T, lower=True).T  48 us
    unnamed x52, local copies, waits for them, and re-layouts  29.9 us
  transfers between devices with their start and end apart: 7, of which 5 were waited for; matrix products, arithmetic and copies ran while one was open for 10% of the time, Pallas kernels for 0%

profile of v1, /device:TPU:0, one launch (start us, length us, event | category | flops | bytes accessed | tf_op | source)
XLA Modules:
  0.0 1105.5 jit_solution(8289677037031417852)
XLA Ops:
  24.8 58.7 %all-reduce.4.cloned.1.call-done = f32[512,512]{1,0:T(8,128)} async-done(((f32[512,512]{1,0:T(8,128)}), f32[512,512]{1,0:T(8,128)}) %all-reduce.4.cloned.1.call-update) | async-done | bytes 1048592 | tf_op jit(solution)/shard_map/psum | solution.py:11
  86.6 11.7 %cholesky.286 = f32[128,128]{1,0:T(8,128)S(1)} custom-call(f32[128,128]{1,0:T(8,128)S(1)} %copy.14), custom_call_target="Cholesky" | custom-call | tf_op jit(solution)/shard_map/jit(cholesky)/cholesky | solution.py:47
  98.4 9.8 custom-call.33
  109.3 11.7 %cholesky.305 = f32[128,128]{1,0:T(8,128)S(1)} custom-call(f32[128,128]{1,0:T(8,128)S(1)} %copy.16), custom_call_target="Cholesky" | custom-call | tf_op jit(solution)/shard_map/jit(cholesky)/cholesky | solution.py:47
  121.1 10.0 custom-call.34
  132.0 11.7 %cholesky.326 = f32[128,128]{1,0:T(8,128)S(1)} custom-call(f32[128,128]{1,0:T(8,128)S(1)} %copy.18), custom_call_target="Cholesky" | custom-call | tf_op jit(solution)/shard_map/jit(cholesky)/cholesky | solution.py:47
  144.3 9.8 custom-call.35
  154.9 12.1 %cholesky.343 = f32[128,128]{1,0:T(8,128)S(1)} custom-call(f32[128,128]{1,0:T(8,128)S(1)} %copy.20), custom_call_target="Cholesky" | custom-call | tf_op jit(solution)/shard_map/jit(cholesky)/cholesky | solution.py:47
  178.9 39.3 %custom-call.36 = f32[4,128,128]{1,2,0:T(8,128)S(1)} custom-call(f32[4,128,128]{2,1,0:T(8,128)S(1)} %get-tuple-element.193), custom_call_target="InvertDiagBlocksLowerTriangular" | custom-call | tf_op jit(solution)/shard_map/jit(_solve_triangular)/triangular_solve | solution.py:31
  245.7 146.3 %all-gather.3.cloned.1.call-done = f32[4096,1024]{1,0:T(8,128)} async-done(((f32[512,1024]{1,0:T(8,128)}), f32[4096,1024]{1,0:T(8,128)}) %all-gather.3.cloned.1.call-update) | async-done | bytes 16777232 | tf_op jit(solution)/shard_map/all_gather | solution.py:55
  392.0 17.5 %constant_dynamic-update-slice_fusion.4 = (f32[512,4096]{1,0:T(8,128)}, f32[512,3584]{1,0:T(8,128)S(1)}) fusion(f32[512,4096]{1,0:T(8,128)} %get-tuple-element.217, f32[4096,1024]{1,0:T(8,128)} %all-gather.3.cloned.1.call-done, f32[128,512]{0,1:T(8,128)S(1)} %fusion.146, f32[128,512]{0,1:T(8,128)S(1)} %copy.23, f32[128,512]{0,1:T(8,128)S(1)} %copy.22, ...), kind=kOutput, calls=%fused_computation.253 | convolution fusion | flops 11280842752 | bytes 30409728 | tf_op jit(solution)/shard_map/dot_general | solution.py:21
  416.3 17.6 %constant_dynamic-update-slice_fusion.3 = (f32[512,4096]{1,0:T(8,128)}, f32[512,3584]{1,0:T(8,128)S(1)}) fusion(f32[512,4096]{1,0:T(8,128)} %select_dynamic-update-slice_fusion.1, f32[4096,1024]{1,0:T(8,128)} %all-gather.3.cloned.1.call-done, f32[128,512]{0,1:T(8,128)S(1)} %fusion.145, f32[128,512]{0,1:T(8,128)S(1)} %copy.27, f32[128,512]{0,1:T(8,128)S(1)} %copy.26, ...), kind=kOutput, calls=%fused_computation.252 | convolution fusion | flops 11278745600 | bytes 30408704 | tf_op jit(solution)/shard_map/dot_general | solution.py:21
  437.9 36.6 %all-reduce.6.cloned.1.call-done = f32[512,512]{0,1:T(8,128)} async-done(((f32[512,512]{0,1:T(8,128)}), f32[512,512]{0,1:T(8,128)}) %all-reduce.6.cloned.1.call-update) | async-done | bytes 1048592 | tf_op jit(solution)/shard_map/psum | solution.py:11
  478.5 11.7 %cholesky.358 = f32[128,128]{1,0:T(8,128)S(1)} custom-call(f32[128,128]{1,0:T(8,128)S(1)} %cholesky.439), custom_call_target="Cholesky" | custom-call | tf_op jit(solution)/shard_map/jit(cholesky)/cholesky | solution.py:47
  490.9 9.8 custom-call.38
  503.4 11.7 %cholesky.377 = f32[128,128]{1,0:T(8,128)S(1)} custom-call(f32[128,128]{1,0:T(8,128)S(1)} %cholesky.443), custom_call_target="Cholesky" | custom-call | tf_op jit(solution)/shard_map/jit(cholesky)/cholesky | solution.py:47
  515.8 10.0 custom-call.39
  527.4 11.7 %cholesky.398 = f32[128,128]{1,0:T(8,128)S(1)} custom-call(f32[128,128]{1,0:T(8,128)S(1)} %cholesky.448), custom_call_target="Cholesky" | custom-call | tf_op jit(solution)/shard_map/jit(cholesky)/cholesky | solution.py:47
  539.8 9.8 custom-call.40
  551.1 11.7 %cholesky.415 = f32[128,128]{1,0:T(8,128)S(1)} custom-call(f32[128,128]{1,0:T(8,128)S(1)} %convolution_subtract_fusion.16), custom_call_target="Cholesky" | custom-call | tf_op jit(solution)/shard_map/jit(cholesky)/cholesky | solution.py:47
  567.4 12.0 %while.25 = (s32[]{:T(128)}, f32[512,512]{1,0:T(8,128)}, s32[4,2]{0,1:T(2,128)S(1)}, f32[4,128,128]{2,1,0:T(8,128)S(1)}, s32[]{:T(128)}) while((s32[]{:T(128)}, f32[512,512]{1,0:T(8,128)}, s32[4,2]{0,1:T(2,128)S(1)}, f32[4,128,128]{2,1,0:T(8,128)S(1)}, s32[]{:T(128)}) %tuple.139), condition=%wide.while_cond.12.clone.1, body=%wide.while_body.12.clone.1.sunk | while | flops 2 | bytes 131189 | solution.py:31
  579.5 39.3 %custom-call.41 = f32[4,128,128]{1,2,0:T(8,128)S(1)} custom-call(f32[4,128,128]{2,1,0:T(8,128)S(1)} %get-tuple-element.195), custom_call_target="InvertDiagBlocksLowerTriangular" | custom-call | tf_op jit(solution)/shard_map/jit(_solve_triangular)/triangular_solve | solution.py:31
  654.9 145.5 %all-gather.5.cloned.1.call-done = f32[4096,1024]{1,0:T(8,128)} async-done(((f32[512,1024]{1,0:T(8,128)}), f32[4096,1024]{1,0:T(8,128)}) %all-gather.5.cloned.1.call-update) | async-done | bytes 16777232 | tf_op jit(solution)/shard_map/all_gather | solution.py:55
  800.4 17.8 %fusion.3 = f32[512,4096]{1,0:T(8,128)} fusion(f32[4096,1024]{1,0:T(8,128)} %all-gather.5.cloned.1.call-done, f32[128,512]{0,1:T(8,128)S(1)} %fusion.155, f32[128,512]{0,1:T(8,128)S(1)} %copy.37, f32[128,512]{0,1:T(8,128)S(1)} %copy.36, f32[128,512]{0,1:T(8,128)S(1)} %copy.35), kind=kOutput, calls=%fused_computation.9 | convolution fusion | flops 12885688320 | bytes 17825792 | tf_op jit(solution)/shard_map/dot_general | solution.py:21
  818.2 20.7 %subtract_subtract_fusion = f32[512,4096]{1,0:T(8,128)} fusion(f32[512,4096]{1,0:T(8,128)} %fusion.3, f32[512,4096]{1,0:T(8,128)} %param.37, f32[4096,1024]{1,0:T(8,128)} %all-gather.3.cloned.1.call-done, f32[128,512]{0,1:T(8,128)S(1)} %fusion.145, f32[128,512]{0,1:T(8,128)S(1)} %copy.27, f32[128,512]{0,1:T(8,128)S(1)} %copy.26, f32[128,512]{0,1:T(8,128)S(1)} %copy.25), kind=kOutput, calls=%fused_computation.4 | convolution fusion | flops 12889882624 | bytes 34603008 | tf_op jit(solution)/shard_map/dot_general | solution.py:21
  847.5 9.0 fusion.37
  865.1 158.0 %collective-permute-done.2 = f32[32,32]{1,0:T(8,128)S(1)} collective-permute-done((f32[32,32]{1,0:T(8,128)S(1)}, f32[32,32]{1,0:T(8,128)S(1)}, u32[]{:S(2)}, u32[]{:S(2)}) %collective-permute-start.2) | collective-permute-done | bytes 4128 | tf_op jit(solution)/shard_map/ppermute | solution.py:17
  1023.1 9.9 fusion.1
  1033.0 10.1 fusion.31
  1047.6 13.4 %fusion.15 = f32[512,4096]{1,0:T(8,128)S(1)} fusion(f32[512,4096]{1,0:T(8,128)S(1)} %bitcast.191, f32[4096,1024]{1,0:T(8,128)} %all-gather.5.cloned.1.call-done, pred[512]{0:T(512)(128)(4,1)S(1)} %fusion.181, f32[128,512]{0,1:T(8,128)S(1)} %copy-done.10, f32[128,512]{0,1:T(8,128)S(1)} %copy-done.8, f32[128,512]{0,1:T(8,128)S(1)} %copy-done.7, ...), kind=kOutput, calls=%fused_computation.25 | convolution fusion | flops 9669443584 | bytes 19923968 | tf_op jit(solution)/shard_map/dot_general | solution.py:21
  1065.7 13.0 %fusion.14 = f32[512,4096]{1,0:T(8,128)S(1)} fusion(f32[512,4096]{1,0:T(8,128)S(1)} %select_dynamic-update-slice_fusion, f32[4096,1024]{1,0:T(8,128)} %all-gather.5.cloned.1.call-done, f32[128,512]{0,1:T(8,128)S(1)} %fusion.155, f32[128,512]{0,1:T(8,128)S(1)} %copy.37, f32[128,512]{0,1:T(8,128)S(1)} %copy.36, f32[128,512]{0,1:T(8,128)S(1)} %copy.35), kind=kOutput, calls=%fused_computation.23 | convolution fusion | flops 9667608576 | bytes 19922944 | tf_op jit(solution)/shard_map/dot_general | solution.py:21
  1078.7 10.4 fusion.48
  (223 shorter events, 176.2 us)
Async XLA Ops:
  7.2 76.3 %all-reduce.4.cloned.1.call-start = ((), (), s32[]{:S(2)}) async-start(), calls=%async_computation | async-start | bytes 2097152 | tf_op jit(solution)/shard_map/psum | solution.py:11
  7.2 7.9 copy-start.3
  15.1 3.4 copy-start.17
  21.8 370.2 %all-gather.3.cloned.1.call-start = ((), (), s32[]{:S(2)}) async-start(), calls=%async_computation.1 | async-start | bytes 18874368 | tf_op jit(solution)/shard_map/all_gather | solution.py:55
  218.2 19.1 %copy-start.11 = (f32[4,128,128]{1,2,0:T(8,128)}, f32[4,128,128]{1,2,0:T(8,128)S(1)}, u32[]{:S(2)}) copy-start(f32[4,128,128]{1,2,0:T(8,128)S(1)} %custom-call.36) | copy-start | bytes 786436
  221.4 0.7 copy-start.14
  241.8 232.7 %all-reduce.6.cloned.1.call-start = ((), (), s32[]{:S(2)}) async-start(), calls=%async_computation.2 | async-start | bytes 2097152 | tf_op jit(solution)/shard_map/psum | solution.py:11
  409.5 3.0 copy-start.1
  416.2 384.1 %all-gather.5.cloned.1.call-start = ((), (), s32[]{:S(2)}) async-start(), calls=%async_computation.3 | async-start | bytes 18874368 | tf_op jit(solution)/shard_map/all_gather | solution.py:55
  433.9 2.9 copy-start.2
  477.5 1.0 copy-start.6
  618.8 12.5 %copy-start.12 = (f32[4,128,128]{1,2,0:T(8,128)}, f32[4,128,128]{1,2,0:T(8,128)S(1)}, u32[]{:S(2)}) copy-start(f32[4,128,128]{1,2,0:T(8,128)S(1)} %custom-call.41) | copy-start | bytes 786436
  637.6 0.7 copy-start.15
  643.9 1.5 copy-start.9
  800.4 61.9 %slice-start.2 = ((s8[8388608]{0:T(1024)(128)(4,1)}), s8[4194304]{0:T(1024)(128)(4,1)S(1)}, s32[]{:S(2)}) async-start(s8[8388608]{0:T(1024)(128)(4,1)} %bitcast.192), calls=%async_computation.6 | async-start | bytes 8388608
  818.2 28.4 %copy-start.18 = (f32[32,32]{1,0:T(8,128)S(1)}, f32[32,32]{1,0:T(8,128)}, u32[]{:S(2)}) copy-start(f32[32,32]{1,0:T(8,128)} %param.40) | copy-start | bytes 12292
  818.2 28.6 %copy-start.4 = (f32[32,4096]{1,0:T(8,128)S(1)}, f32[32,4096]{1,0:T(8,128)}, u32[]{:S(2)}) copy-start(f32[32,4096]{1,0:T(8,128)} %copy.107) | copy-start | bytes 1572868
  818.2 44.1 %slice-start.3 = ((s8[8388608]{0:T(1024)(128)(4,1)}), s8[4194304]{0:T(1024)(128)(4,1)S(1)}, s32[]{:S(2)}) async-start(s8[8388608]{0:T(1024)(128)(4,1)} %bitcast.192), calls=%async_computation.7 | async-start | bytes 8388608
  838.9 17.7 %copy-start.13 = (f32[4,128,128]{1,2,0:T(8,128)S(1)}, f32[4,128,128]{1,2,0:T(8,128)}, u32[]{:S(2)}) copy-start(f32[4,128,128]{1,2,0:T(8,128)} %copy-done.12) | copy-start | bytes 786436
  838.9 250.2 %collective-permute-start = (f32[512,4096]{1,0:T(8,128)}, f32[512,4096]{1,0:T(8,128)}, u32[]{:S(2)}, u32[]{:S(2)}) collective-permute-start(f32[512,4096]{1,0:T(8,128)} %subtract_subtract_fusion), channel_id=1, source_target_pairs={{0,8},{8,16},{16,24},{1,9},{9,17},{17,25},{2,10},{10,18},{18,26},{... | collective-permute-start | bytes 25165832 | tf_op jit(solution)/shard_map/ppermute | solution.py:17
  856.6 176.4 %copy-start.16 = (f32[32,4096]{1,0:T(8,128)S(1)}, f32[32,4096]{1,0:T(8,128)}, u32[]{:S(2)}) copy-start(f32[32,4096]{1,0:T(8,128)} %param.39) | copy-start | bytes 1572868
  861.0 162.1 %collective-permute-start.2 = (f32[32,32]{1,0:T(8,128)S(1)}, f32[32,32]{1,0:T(8,128)S(1)}, u32[]{:S(2)}, u32[]{:S(2)}) collective-permute-start(f32[32,32]{1,0:T(8,128)S(1)} %convolution_subtract_fusion.18), channel_id=1, source_target_pairs={{0,8},{8,16},{16,24},{1,9},{9,17},{17,25},{2,10},{10,18},{18,26},{... | collective-permute-start | bytes 12296 | tf_op jit(solution)/shard_map/ppermute | solution.py:17
  865.1 182.5 %slice-start = ((s8[8388608]{0:T(1024)(128)(4,1)}), s8[4194304]{0:T(1024)(128)(4,1)S(1)}, s32[]{:S(2)}) async-start(s8[8388608]{0:T(1024)(128)(4,1)} %bitcast.190), calls=%async_computation.4 | async-start | bytes 8388608
  865.1 182.5 %copy-start.7 = (f32[128,512]{0,1:T(8,128)S(1)}, f32[128,512]{0,1:T(8,128)}, u32[]{:S(2)}) copy-start(f32[128,512]{0,1:T(8,128)} %copy.32) | copy-start | bytes 786436
  865.1 182.5 %copy-start.8 = (f32[128,512]{0,1:T(8,128)S(1)}, f32[128,512]{0,1:T(8,128)}, u32[]{:S(2)}) copy-start(f32[128,512]{0,1:T(8,128)} %copy.33) | copy-start | bytes 786436
  865.1 182.5 %copy-start.10 = (f32[128,512]{0,1:T(8,128)S(1)}, f32[128,512]{0,1:T(8,128)}, u32[]{:S(2)}) copy-start(f32[128,512]{0,1:T(8,128)} %copy-done.9) | copy-start | bytes 786436
  1033.0 14.6 %slice-start.1 = ((s8[8388608]{0:T(1024)(128)(4,1)}), s8[4194304]{0:T(1024)(128)(4,1)S(1)}, s32[]{:S(2)}) async-start(s8[8388608]{0:T(1024)(128)(4,1)} %bitcast.190), calls=%async_computation.5 | async-start | bytes 8388608
  1043.1 46.0 %collective-permute-start.1 = (f32[32,4096]{1,0:T(8,128)S(1)}, f32[32,4096]{1,0:T(8,128)S(1)}, u32[]{:S(2)}, u32[]{:S(2)}) collective-permute-start(f32[32,4096]{1,0:T(8,128)S(1)} %fusion.31), channel_id=1, source_target_pairs={{0,8},{8,16},{16,24},{1,9},{9,17},{17,25},{2,10},{10,18},{18,26},{... | collective-permute-start | bytes 1572872 | tf_op jit(solution)/shard_map/ppermute | solution.py:17
  1078.7 18.4 %copy-start = (f32[512,4096]{1,0:T(8,128)}, f32[512,4096]{1,0:T(8,128)S(1)}, u32[]{:S(2)}) copy-start(f32[512,4096]{1,0:T(8,128)S(1)} %fusion.14) | copy-start | bytes 25165828
  1089.1 8.0 copy-start.5
Sparse Core Ops, SparseCore 0:
  22.0 61.4 all-reduce.3
  241.9 150.0 all-gather.2
  416.4 58.0 all-reduce.5
  650.3 150.0 all-gather.4
